TPU v7x, 256 devices: a whole 4x4x8 slice. The times are simulated.
256 devices in a mesh: dp: 8 (over x_hi, y), tp: 32 (over x_lo, z, core).
Axes of the slice: x: 4 (x_hi: 2, x_lo: 2; x = x_hi * 2 + x_lo), y: 4, z: 8, core: 2. Of those that a mesh axis runs over, the one named last changes fastest.
Arguments:
- hidden: bfloat16 [6144, 2880], P(('dp', 'tp')), parts along dimension 0, may hold values from -6 to 6
- attn_gain: float32 [2880], replicated, may hold values from 0.1 to 1.9
- w_query: bfloat16 [2880, 4096], P(None, 'tp'), may hold values from -0.109375 to 0.109375
- w_keyval: bfloat16 [2880, 1024], P(None, 'tp'), may hold values from -0.109375 to 0.109375
- w_out: bfloat16 [4096, 2880], P('tp'), may hold values from -0.09375 to 0.09375
- cache_keys: bfloat16 [256, 2048, 512], P(('dp', 'tp')), parts along dimension 0, may hold values from -70 to 70
- cache_values: bfloat16 [256, 2048, 512], P(('dp', 'tp')), parts along dimension 0, may hold values from -6 to 6
- cache_lens: int32 [256], P(('dp', 'tp')), parts along dimension 0, may hold values from 256 to 2048, as said below
- parents: int32 [256, 24], P(('dp', 'tp')), parts along dimension 0, may hold values from 0 to 23, as said below
- accepted: int32 [256], P(('dp', 'tp')), parts along dimension 0, may hold values from 0 to 23, as said below
- moe_gain: float32 [2880], replicated, may hold values from 0.1 to 1.9
- w_router: bfloat16 [2880, 32], replicated, may hold values from -0.109375 to 0.109375
- routes: int32 [6144, 4], P('dp'), parts along dimension 0, may hold values from 0 to 31, all different within a row; in each aligned block of 768 rows (0 to 767, 768 to 1535, ...) at most 192 rows name the same one
- w_gate: bfloat16 [11520, 2880], P('tp'), may hold values from -0.109375 to 0.109375
- w_up: bfloat16 [11520, 2880], P('tp'), may hold values from -0.109375 to 0.109375
- w_down: bfloat16 [11520, 2880], P('tp'), may hold values from -0.109375 to 0.109375
Outputs:
- layer_out: bfloat16 [6144, 2880], P(('dp', 'tp')), parts along dimension 0
- accepted_kv: bfloat16 [256, 8, 1024], P(('dp', 'tp')), parts along dimension 0
There are 8 independent parts, one for each index of `dp`. A program takes and returns all parts, laid end to end along the dimension named above; an argument that names none is the same for every part. Nothing has to cross between parts.
Inputs may be any that keep to these rules, and one draw needn't show every extreme that they name: `cache_lens`: 2048 for at least one request of every part. `parents`: node 0 names itself; every other node names a node of smaller index; no path from node 0 holds more than 8 nodes, and every tree has one of exactly 8. The path from node 0 to the accepted node holds at most 8 nodes, exactly 8 for at least one request of every part. `routes`: each token names 4 different experts; at most 192 tokens of a part name any one expert, a bound that some block reaches.
All inputs are finite; a program needn't handle non-finite values.
Results may differ from a plain program's by a relative error of at most 0.012.
The roundings to bfloat16 on the way count: a program that leaves them out, or rounds other values in their place, can miss the bound.
Values may be sent and summed in bfloat16 or wider, within the bound.
A program may use at most 128 MiB of HBM per device.

v0:
```python
import math

import jax
import jax.numpy as jnp
from jax import lax
from jax.sharding import PartitionSpec as P

HEADS = 64
HEAD_DIM = 64
EXPERT_HID = 2880
DEPTH = 8


THETA = 150000.0
SWIGLU_ALPHA = 1.702
EPSILON = 1e-05


def rms_norm(values, gain):
    floats = values.astype(jnp.float32)
    mean_sq = jnp.mean(floats * floats, axis=-1, keepdims=True)
    return (floats * lax.rsqrt(mean_sq + EPSILON) * gain).astype(jnp.bfloat16)


def tree_paths(parent_row, depth_limit):
    count = parent_row.shape[0]
    identity = jnp.eye(count, dtype=jnp.bool_)
    ancestry = identity
    for level in range(depth_limit):
        ancestry = identity | jnp.take(ancestry, parent_row, axis=0)
    depths = jnp.sum(ancestry.astype(jnp.int32), axis=1) - 1
    return (ancestry, depths)


def rotate(values, positions):
    half = values.shape[-1] // 2
    steps_f = jnp.arange(half).astype(jnp.float32)
    inverse = jnp.exp(steps_f * (-2.0 * math.log(THETA) / values.shape[-1]))
    angles = positions[:, None] * inverse[None, :]
    cosine = jnp.cos(angles)[:, None, :]
    sine = jnp.sin(angles)[:, None, :]
    first = values[..., :half].astype(jnp.float32)
    second = values[..., half:].astype(jnp.float32)
    turned = jnp.concatenate(
        [first * cosine - second * sine, second * cosine + first * sine], axis=-1
    )
    return turned.astype(jnp.bfloat16)


def prepare(query, keyval, length, parent_row, depth_limit):
    draft, heads, head_dim = query.shape
    kv_width = keyval.shape[1] // 2
    kv_heads = kv_width // head_dim
    ancestry, depths = tree_paths(parent_row, depth_limit)
    positions = (length + depths).astype(jnp.float32)
    query_rot = rotate(query, positions)
    new_keys = rotate(keyval[:, :kv_width].reshape(draft, kv_heads, head_dim), positions)
    new_values = keyval[:, kv_width:].reshape(draft, kv_heads, head_dim)
    grouped = query_rot.reshape(draft, kv_heads, heads // kv_heads, head_dim)
    draft_scores = jnp.einsum(
        "jgqd,kgd->gqjk", grouped, new_keys, preferred_element_type=jnp.float32
    ) * (1.0 / math.sqrt(head_dim))
    draft_scores = jnp.where(ancestry[None, None], draft_scores, -jnp.inf)
    return (grouped, new_keys, new_values, ancestry, depths, draft_scores)


def accept_rows(new_keys, new_values, ancestry, depths, leaf, depth_limit):
    draft = depths.shape[0]
    selector = ancestry[leaf][None, :] & (depths[None, :] == jnp.arange(depth_limit)[:, None])
    new_rows = jnp.concatenate([new_keys.reshape(draft, -1), new_values.reshape(draft, -1)], axis=1)
    return jnp.dot(
        selector.astype(jnp.bfloat16), new_rows, preferred_element_type=jnp.float32
    ).astype(jnp.bfloat16)


def finish(weighted, total, draft):
    return (
        (weighted / jnp.transpose(total, (2, 0, 1))[..., None])
        .astype(jnp.bfloat16)
        .reshape(draft, -1)
    )


def attend_padded(query, keyval, keys_cache, values_cache, length, parent_row, leaf, depth_limit):
    draft, heads, head_dim = query.shape
    grouped, new_keys, new_values, ancestry, depths, draft_scores = prepare(
        query, keyval, length, parent_row, depth_limit
    )
    slots = keys_cache.shape[0]
    kv_heads = new_keys.shape[1]
    cache_k = keys_cache.reshape(slots, kv_heads, head_dim)
    cache_v = values_cache.reshape(slots, kv_heads, head_dim)
    cache_scores = jnp.einsum(
        "jgqd,pgd->gqjp", grouped, cache_k, preferred_element_type=jnp.float32
    ) * (1.0 / math.sqrt(head_dim))
    live = jnp.arange(slots) < length
    cache_scores = jnp.where(live[None, None, None], cache_scores, -jnp.inf)
    top = jnp.maximum(jnp.max(draft_scores, axis=-1), jnp.max(cache_scores, axis=-1))
    draft_exp = jnp.exp(draft_scores - top[..., None])
    cache_exp = jnp.exp(cache_scores - top[..., None])
    total = jnp.sum(draft_exp, axis=-1) + jnp.sum(cache_exp, axis=-1)
    weighted = jnp.einsum(
        "gqjk,kgd->jgqd",
        draft_exp.astype(jnp.bfloat16),
        new_values,
        preferred_element_type=jnp.float32,
    )
    weighted = weighted + jnp.einsum(
        "gqjp,pgd->jgqd",
        cache_exp.astype(jnp.bfloat16),
        cache_v,
        preferred_element_type=jnp.float32,
    )
    return (
        finish(weighted, total, draft),
        accept_rows(new_keys, new_values, ancestry, depths, leaf, depth_limit),
    )


def gate_weights(inputs, router, routes):
    logits = jnp.dot(inputs, router, preferred_element_type=jnp.float32)
    onehot = routes[:, :, None] == jnp.arange(router.shape[1])[None, None, :]
    picked = jnp.sum(jnp.where(onehot, logits[:, None, :], 0.0), axis=2)
    return jax.nn.softmax(picked, axis=1).astype(jnp.bfloat16)


def expert_slots(inputs, weights, routes, expert, gate_rows, up_rows, down_rows, capacity):
    count = inputs.shape[0]
    match = routes == expert
    hits = jnp.any(match, axis=1)
    gate_of = jnp.sum(jnp.where(match, weights.astype(jnp.float32), 0.0), axis=1)
    slot_ids = jnp.cumsum(hits.astype(jnp.int32)) - 1
    target = jnp.where(hits, slot_ids, capacity)
    index = jnp.full((capacity,), count, jnp.int32).at[target].set(jnp.arange(count), mode="drop")
    valid = index < count
    safe = jnp.minimum(index, count - 1)
    picked = inputs[safe]
    gate_val = lax.dot_general(
        picked, gate_rows, (((1,), (1,)), ((), ())), preferred_element_type=jnp.float32
    )
    up_val = lax.dot_general(
        picked, up_rows, (((1,), (1,)), ((), ())), preferred_element_type=jnp.float32
    )
    active = (gate_val * jax.nn.sigmoid(SWIGLU_ALPHA * gate_val) * (up_val + 1.0)).astype(
        jnp.bfloat16
    )
    result = jnp.dot(active, down_rows, preferred_element_type=jnp.float32)
    scale_rows = jnp.where(valid, gate_of[safe], 0.0)
    return (result * scale_rows[:, None], index)


def local(
    hidden,
    attn_gain,
    w_query,
    w_keyval,
    w_out,
    cache_keys,
    cache_values,
    cache_lens,
    parents,
    accepted,
    moe_gain,
    w_router,
    routes,
    w_gate,
    w_up,
    w_down,
):
    devices = lax.axis_size("tp")
    index_me = lax.axis_index("tp")
    rows = hidden.shape[0]
    normed = rms_norm(hidden, attn_gain)
    local_query = w_query.shape[1]
    both_weights = jnp.concatenate([w_query, w_keyval], axis=1)
    projected = jnp.dot(
        lax.all_gather(normed, "tp", axis=0, tiled=True),
        both_weights,
        preferred_element_type=jnp.float32,
    ).astype(jnp.bfloat16)
    width = projected.shape[1]
    gathered_cols = lax.all_to_all(projected, "tp", split_axis=0, concat_axis=1, tiled=True)
    gathered_cols = gathered_cols.reshape(rows, devices, width)
    requests = cache_lens.shape[0]
    draft = parents.shape[1]
    query = gathered_cols[:, :, :local_query].reshape(requests, draft, HEADS, HEAD_DIM)
    keyval = gathered_cols[:, :, local_query:].reshape(
        requests, draft, devices * (width - local_query)
    )

    def per_request(items):
        return attend_padded(*items, DEPTH)

    attended, accepted_kv = lax.map(
        per_request, (query, keyval, cache_keys, cache_values, cache_lens, parents, accepted)
    )
    attended = attended.reshape(rows, HEADS * HEAD_DIM)
    head_cols = lax.all_to_all(attended, "tp", split_axis=1, concat_axis=0, tiled=True)
    attn_sum = lax.psum_scatter(
        jnp.dot(head_cols, w_out, preferred_element_type=jnp.float32),
        "tp",
        scatter_dimension=0,
        tiled=True,
    )
    middle = (hidden.astype(jnp.float32) + attn_sum).astype(jnp.bfloat16)
    moe_in = rms_norm(middle, moe_gain)
    all_inputs = lax.all_gather(moe_in, "tp", axis=0, tiled=True)
    all_weights = gate_weights(all_inputs, w_router, routes)
    units = w_down.shape[0]
    expert = index_me * units // EXPERT_HID
    count = all_inputs.shape[0]
    capacity = 2 * count * routes.shape[1] // w_router.shape[1]
    slot_rows, slot_index = expert_slots(
        all_inputs, all_weights, routes, expert, w_gate, w_up, w_down, capacity
    )
    term = (
        jnp.zeros((count, all_inputs.shape[1]), jnp.float32)
        .at[slot_index]
        .add(slot_rows, mode="drop")
    )
    mixed = lax.psum_scatter(
        term.astype(jnp.bfloat16), "tp", scatter_dimension=0, tiled=True
    ).astype(jnp.float32)
    layer_out = (middle.astype(jnp.float32) + mixed).astype(jnp.bfloat16)
    return (layer_out, accepted_kv)


def solution(mesh):
    return jax.shard_map(
        local,
        mesh=mesh,
        in_specs=(
            P(("dp", "tp"), None),
            P(),
            P(None, "tp"),
            P(None, "tp"),
            P("tp", None),
            P(("dp", "tp"), None, None),
            P(("dp", "tp"), None, None),
            P(("dp", "tp")),
            P(("dp", "tp"), None),
            P(("dp", "tp")),
            P(),
            P(),
            P("dp", None),
            P("tp", None),
            P("tp", None),
            P("tp", None),
        ),
        out_specs=(P(("dp", "tp"), None), P(("dp", "tp"), None, None)),
        check_vma=False,
    )
```

profile of v0, /device:TPU:8, one launch (start us, length us, event | category | flops | bytes accessed | tf_op | source)
XLA Modules:
  0.0 524.9 jit_solution(3965002201816754766)
XLA Ops:
  7.2 1.2 fusion.39
  8.4 1.7 fusion.41
  10.1 0.7 compare_select_fusion.3
  10.8 0.6 gather_fusion.2
  11.4 0.7 compare_and_fusion
  12.1 0.6 gather_fusion.3
  12.8 0.6 gather_fusion.4
  13.5 0.6 gather_fusion.5
  14.1 0.6 gather_fusion.6
  14.8 0.6 gather_fusion.7
  15.4 0.6 gather_fusion.8
  16.1 0.6 gather_fusion.9
  17.3 1.3 copy.138
  18.9 61.4 %all-gather.3.cloned.1.call-done = bf16[768,2880]{1,0:T(8,128)(2,1)} async-done(((bf16[24,2880]{1,0:T(8,128)(2,1)}), bf16[768,2880]{1,0:T(8,128)(2,1)}) %all-gather.3.cloned.1.call-update) | async-done | bytes 4423696 | tf_op jit(solution)/shard_map/all_gather | solution.py:177
  80.2 4.2 fusion.17
  84.4 0.9 copy.139
  85.3 6.3 %all-to-all-start = ((bf16[32,24,160]{2,1,0:T(8,128)(2,1)}), bf16[32,24,160]{2,1,0:T(8,128)(2,1)S(1)}, u32[]{:S(2)}, u32[]{:S(2)}) async-start(bf16[32,24,160]{2,1,0:T(8,128)(2,1)} %bitcast), calls=%async_computation | async-start | bytes 786432 | tf_op jit(solution)/shard_map/all_to_all | solution.py:182
  91.9 3.9 copy.151
  95.8 0.7 copy.141
  96.5 4.0 copy.157
  100.4 0.5 broadcast_add_fusion
  101.1 6.4 %all-to-all-done = bf16[32,24,160]{2,1,0:T(8,128)(2,1)S(1)} async-done(((bf16[32,24,160]{2,1,0:T(8,128)(2,1)}), bf16[32,24,160]{2,1,0:T(8,128)(2,1)S(1)}, u32[]{:S(2)}, u32[]{:S(2)}) %all-to-all-start) | async-done | bytes 245792 | tf_op jit(solution)/shard_map/all_to_all | solution.py:182
  108.4 0.9 fusion.26
  109.6 1.2 copy.170
  111.0 8.0 %bitcast_reduce_fusion = (f32[8,8,24]{1,2,0:T(8,128)S(1)}, f32[8,24,8,2048]{3,2,1,0:T(8,128)}) fusion(pred[2048]{0:T(1024)(128)(4,1)S(1)} %iota_compare_fusion.2, bf16[2048,8,64,1]{0,2,3,1:T(8,128)(2,1)} %bitcast.92, bf16[24,8,8,64]{3,0,2,1:T(8,128)(2,1)S(1)} %pad_maximum_fusion), kind=kOutput, calls=%fused_computation.13 | convolution fusion | flops 412088832 | bytes 14884864 | tf_op jit(solution)/shard_map/while/body/eval_jaxpr/jgqd,pgd->gqjp/dot_general | solution.py:93
  119.7 1.5 fusion.83
  121.3 7.2 %fusion.1 = f32[8,8,24]{1,2,0:T(8,128)S(1)} fusion(f32[8,24,8,2048]{3,2,1,0:T(8,128)} %get-tuple-element.58, f32[8,8,24]{1,2,0:T(8,128)S(1)} %copy.156, pred[2048]{0:T(1024)(128)(4,1)} %copy-done.4), kind=kLoop, calls=%fused_computation.16 | loop fusion | flops 12581376 | bytes 12597248 | tf_op jit(solution)/shard_map/while/body/eval_jaxpr/reduce_sum | solution.py:101
  128.8 8.4 %fusion.3 = f32[8,8,24,64]{3,1,2,0:T(8,128)} fusion(bf16[2048,8,64,1]{0,2,3,1:T(8,128)(2,1)} %bitcast.93, f32[8,24,8,2048]{3,2,1,0:T(8,128)} %get-tuple-element.58, f32[8,8,24]{1,2,0:T(8,128)S(1)} %copy.156, pred[2048]{0:T(1024)(128)(4,1)S(1)} %copy-done.5), kind=kOutput, calls=%fused_computation.18 | convolution fusion | flops 415236096 | bytes 15081472 | tf_op jit(solution)/shard_map/while/body/eval_jaxpr/gqjp,pgd->jgqd/dot_general | solution.py:108
  137.2 1.6 fusion.16
  139.2 14.8 %all_to_all.35 = bf16[24,32,128]{2,0,1:T(8,128)(2,1)S(1)} all-to-all(bf16[24,32,128]{2,0,1:T(8,128)(2,1)S(1)} %copy.161), channel_id=1, replica_groups=mesh['dp'=8,'tp'=32] {'tp'}, dimensions={1} | all-to-all | bytes 393216 | tf_op jit(solution)/shard_map/all_to_all | solution.py:198
  154.0 5.9 %fusion.84 = f32[768,2880]{1,0:T(8,128)} fusion(bf16[768,128]{1,0:T(8,128)(2,1)S(1)} %bitcast.98, bf16[128,2880]{0,1:T(8,128)(2,1)} %param.22), kind=kOutput, calls=%fused_computation.145 | convolution fusion | flops 566231040 | bytes 9781248 | tf_op jit(solution)/shard_map/dot_general | solution.py:200
  160.0 127.7 %reduce-scatter.9.cloned.1.call-done = f32[24,2880]{1,0:T(8,128)} async-done(((f32[768,2880]{1,0:T(8,128)}), f32[24,2880]{1,0:T(8,128)}) %reduce-scatter.9.cloned.1.call-update) | async-done | bytes 276496
  287.7 1.1 fusion.43
  288.8 0.8 fusion.45
  289.9 63.0 %all-gather.5.cloned.1.call-done = bf16[768,2880]{1,0:T(8,128)(2,1)} async-done(((bf16[24,2880]{1,0:T(8,128)(2,1)}), bf16[768,2880]{1,0:T(8,128)(2,1)}) %all-gather.5.cloned.1.call-update) | async-done | bytes 4423696 | tf_op jit(solution)/shard_map/all_gather | solution.py:207
  352.9 3.6 fusion.86
  356.7 0.3 reduce-window.9
  357.3 3.4 scatter_custom_fusion
  360.7 1.2 gather_fusion.1
  361.9 5.3 %gather_fusion = bf16[192,2880]{1,0:T(8,128)(2,1)S(1)} fusion(bf16[768,2880]{1,0:T(8,128)(2,1)} %all-gather.5.cloned.1.call-done, s32[1024]{0:T(1024)S(1)} %pad_clamp_fusion), kind=kCustom, calls=%fused_computation.8 | custom fusion | bytes 2212608 | tf_op jit(solution)/shard_map/gather | solution.py:137
  367.3 3.2 fusion.85
  370.5 4.8 convolution_multiply_fusion
  375.3 8.7 %scatter_custom_fusion.1 = f32[768,2880]{1,0:T(8,128)} fusion(s32[192]{0:T(256)S(1)} %get-tuple-element.50, f32[192,2880]{1,0:T(8,128)} %convolution_multiply_fusion, f32[]{:T(128)} %constant.29.clone.1), kind=kCustom, calls=%fused_computation.20 | custom fusion | flops 552960 | bytes 8847872 | tf_op jit(solution)/shard_map/scatter-add | solution.py:219
  384.0 6.2 %convert_element_type.133 = bf16[768,2880]{1,0:T(8,128)(2,1)} convert(f32[768,2880]{1,0:T(8,128)} %scatter_custom_fusion.1) | non-fusion elementwise | flops 2211840 | bytes 13271040 | tf_op jit(solution)/shard_map/convert_element_type | solution.py:222
  390.9 0.7 dynamic-slice_bitcast_fusion
  391.7 0.7 fusion.22
  392.4 124.3 %reduce-scatter.11.cloned.1.call-done = bf16[24,2880]{1,0:T(8,128)(2,1)} async-done(((bf16[768,2880]{1,0:T(8,128)(2,1)}), bf16[24,2880]{1,0:T(8,128)(2,1)}) %reduce-scatter.11.cloned.1.call-update) | async-done | bytes 138256
  516.7 1.6 fusion.46
  (84 shorter events, 5.1 us)
Async XLA Ops:
  7.2 363.3 %copy-start = (bf16[360,2880]{1,0:T(8,128)(2,1)S(1)}, bf16[360,2880]{1,0:T(8,128)(2,1)}, u32[]{:S(2)}) copy-start(bf16[360,2880]{1,0:T(8,128)(2,1)} %param.33) | copy-start | bytes 6220804
  7.2 73.1 %all-gather.3.cloned.1.call-start = ((), (), s32[]{:S(2)}) async-start(), calls=%async_computation.4 | async-start | bytes 4663296 | tf_op jit(solution)/shard_map/all_gather | solution.py:177
  18.7 92.3 %copy-start.4 = (pred[2048]{0:T(1024)(128)(4,1)}, pred[2048]{0:T(1024)(128)(4,1)S(1)}, u32[]{:S(2)}) copy-start(pred[2048]{0:T(1024)(128)(4,1)S(1)} %iota_compare_fusion.2) | copy-start | bytes 6148
  18.9 77.0 %copy-start.7 = (pred[24,24]{1,0:T(8,128)(4,1)}, pred[24,24]{1,0:T(8,128)(4,1)S(1)}, u32[]{:S(2)}) copy-start(pred[24,24]{1,0:T(8,128)(4,1)S(1)} %get-tuple-element.28) | copy-start | bytes 1732
  85.3 22.1 %all-to-all-start = ((bf16[32,24,160]{2,1,0:T(8,128)(2,1)}), bf16[32,24,160]{2,1,0:T(8,128)(2,1)S(1)}, u32[]{:S(2)}, u32[]{:S(2)}) async-start(bf16[32,24,160]{2,1,0:T(8,128)(2,1)} %bitcast), calls=%async_computation | async-start | bytes 786432 | tf_op jit(solution)/shard_map/all_to_all | solution.py:182
  91.6 196.1 %reduce-scatter.9.cloned.1.call-start = ((), (), s32[]{:S(2)}) async-start(), calls=%async_computation.6 | async-start | bytes 9326592
  121.3 7.5 %copy-start.5 = (pred[2048]{0:T(1024)(128)(4,1)S(1)}, pred[2048]{0:T(1024)(128)(4,1)}, u32[]{:S(2)}) copy-start(pred[2048]{0:T(1024)(128)(4,1)} %copy-done.4) | copy-start | bytes 6148
  159.9 127.8 %copy-start.1 = (bf16[24,2880]{1,0:T(8,128)(2,1)S(1)}, bf16[24,2880]{1,0:T(8,128)(2,1)}, u32[]{:S(2)}) copy-start(bf16[24,2880]{1,0:T(8,128)(2,1)} %param.18) | copy-start | bytes 414724
  159.9 128.9 %copy-start.6 = (f32[2880]{0:T(1024)S(1)}, f32[2880]{0:T(1024)}, u32[]{:S(2)}) copy-start(f32[2880]{0:T(1024)} %param.28) | copy-start | bytes 34564
  159.9 193.0 %copy-start.2 = (bf16[2880,32]{0,1:T(8,128)(2,1)S(1)}, bf16[2880,32]{0,1:T(8,128)(2,1)}, u32[]{:S(2)}) copy-start(bf16[2880,32]{0,1:T(8,128)(2,1)} %param.29) | copy-start | bytes 552964
  159.9 196.6 %copy-start.3 = (s32[768,4]{0,1:T(4,128)S(1)}, s32[768,4]{0,1:T(4,128)}, u32[]{:S(2)}) copy-start(s32[768,4]{0,1:T(4,128)} %param.30) | copy-start | bytes 36868
  159.9 193.0 %all-gather.5.cloned.1.call-start = ((), (), s32[]{:S(2)}) async-start(), calls=%async_computation.5 | async-start | bytes 4663296 | tf_op jit(solution)/shard_map/all_gather | solution.py:207
  289.6 227.1 %reduce-scatter.11.cloned.1.call-start = ((), (), s32[]{:S(2)}) async-start(), calls=%async_computation.7 | async-start | bytes 4663296
  390.2 1.5 copy-start.8
Sparse Core Ops, SparseCore 0:
  10.4 69.7 all-gather.2
  160.1 127.5 reduce-scatter.8
  290.1 62.7 all-gather.4
  390.4 126.3 reduce-scatter.10
where the time goes:
time: 526 us; the launch traced here: 525 us
  waiting for transfers between devices  383 us (73%)
  matrix products  41.8 us (8%)
  other arithmetic  33.4 us (6%)
  local copies, waits for them, and re-layouts  29.8 us (6%)
  between operations  15.5 us (3%)
  blocking collectives  14.8 us (3%)
  starting transfers between devices  6.85 us (1%)
    unnamed x6, waiting for transfers between devices  252 us
    all_gather x1, waiting for transfers between devices, local(): all_inputs = lax.all_gather(moe_in, 'tp', axis=0, tiled=True)  63 us
    all_gather x1, waiting for transfers between devices, local(): lax.all_gather(normed, 'tp', axis=0, tiled=True)  61.4 us
    all_to_all x1, blocking collectives, local(): lax.all_to_all(attended, 'tp', split_axis=1, concat_axis=0, tiled=True)  14.8 us
  transfers between devices with their start and end apart: 5, of which 5 were waited for; matrix products, arithmetic and copies ran while one was open for 4% of the time, Pallas kernels for 0%

commit v1 on v0

--- a/solution.py
+++ b/solution.py
@@ -1,8 +1,11 @@
+import functools
 import math
 
 import jax
 import jax.numpy as jnp
 from jax import lax
+from jax.experimental import pallas as pl
+from jax.experimental.pallas import tpu as pltpu
 from jax.sharding import PartitionSpec as P
 
 HEADS = 64
@@ -15,11 +18,471 @@
 SWIGLU_ALPHA = 1.702
 EPSILON = 1e-05
 
-
-def rms_norm(values, gain):
-    floats = values.astype(jnp.float32)
-    mean_sq = jnp.mean(floats * floats, axis=-1, keepdims=True)
-    return (floats * lax.rsqrt(mean_sq + EPSILON) * gain).astype(jnp.bfloat16)
+MESH = pl.DeviceIdType.MESH
+RING = 8
+OFFSETS = (0, 1, -1, 2, -2, 3, -3, 4)
+MIRROR = (0, 2, 1, 4, 3, 6, 5, 7)
+LEVELS = ((0,), (1, 2), (3, 4), (5, 6), (7,))
+
+
+def split_of(width):
+    return (width // 2) // 128 * 128
+
+
+class Place:
+    def __init__(self):
+        self.t = lax.axis_index("tp")
+        self.c = lax.rem(self.t, 2)
+        self.z = lax.rem(self.t // 2, RING)
+        self.x = self.t // (2 * RING)
+        self.forward = 1 - 2 * self.c
+
+    def at(self, row, offset, core=None):
+        z = lax.rem(self.z + self.forward * offset + 2 * RING, RING)
+        x = self.x if row == 0 else 1 - self.x
+        return (x * RING + z) * 2 + (self.c if core is None else core)
+
+    def neighbours(self):
+        return (self.at(0, 1), self.at(0, -1), self.at(1, 0), self.at(0, 0, 1 - self.c))
+
+
+def greet(partners):
+    barrier = pltpu.get_barrier_semaphore()
+    for partner in partners:
+        pl.semaphore_signal(barrier, inc=1, device_id={"tp": partner}, device_id_type=MESH)
+    pl.semaphore_wait(barrier, len(partners))
+
+
+def greet_all(place, count):
+    barrier = pltpu.get_barrier_semaphore()
+
+    def one(j, carry):
+        pl.semaphore_signal(
+            barrier, inc=1, device_id={"tp": lax.rem(place.t + j, count)}, device_id_type=MESH
+        )
+        return carry
+
+    lax.fori_loop(1, count, one, 0)
+    pl.semaphore_wait(barrier, count - 1)
+
+
+def remote(src, dst, send_sem, recv_sem, target):
+    return pltpu.make_async_remote_copy(
+        src_ref=src,
+        dst_ref=dst,
+        send_sem=send_sem,
+        recv_sem=recv_sem,
+        device_id={"tp": target},
+        device_id_type=MESH,
+    )
+
+
+def gather_sems():
+    dma = pltpu.SemaphoreType.DMA
+    return [dma((3, 8)), dma((3, 8)), dma((9,)), dma((9,)), dma((4, 8)), dma((4, 8))]
+
+
+def gather_rows(place, low, high, sems):
+    z_send, z_recv, x_send, x_recv, c_send, c_recv = sems
+    streams = ((low, 0), (low, 1), (high, 0))
+    sibling = place.at(0, 0, 1 - place.c)
+    across = place.at(1, 0)
+    sent = []
+
+    def start(copy):
+        copy.start()
+        sent.append(copy)
+
+    def ring_copy(s, slot, block, target):
+        ref = streams[s][0]
+        return remote(ref.at[block], ref.at[block], z_send.at[s, slot], z_recv.at[s, slot], target)
+
+    def ring_send(s, offset, direction):
+        landed = offset - direction
+        slot = OFFSETS.index(4 if landed == -4 else landed)
+        block = place.at(streams[s][1], offset)
+        start(ring_copy(s, slot, block, place.at(0, direction)))
+
+    def ring_wait(s, slot):
+        block = place.at(streams[s][1], OFFSETS[slot])
+        ring_copy(s, slot, block, place.at(0, 1)).wait_recv()
+
+    def across_copy(slot, ref, block):
+        return remote(ref.at[block], ref.at[block], x_send.at[slot], x_recv.at[slot], across)
+
+    def to_sibling(ref, row, slot):
+        q = (0 if ref is low else 2) + row
+        block = place.at(row, OFFSETS[slot])
+        over = MIRROR[slot]
+        start(
+            remote(ref.at[block], ref.at[block], c_send.at[q, over], c_recv.at[q, over], sibling)
+        )
+
+    mine = place.t
+    start(across_copy(8, low, mine))
+    for s in (0, 2):
+        for direction in (1, -1):
+            ring_send(s, 0, direction)
+    start(across_copy(0, high, mine))
+    to_sibling(low, 0, 0)
+    to_sibling(high, 0, 0)
+    across_copy(8, low, across).wait_recv()
+    for direction in (1, -1):
+        ring_send(1, 0, direction)
+    to_sibling(low, 1, 0)
+    for level in range(1, 5):
+        for s in (0, 2, 1):
+            ref, row = streams[s]
+            for slot in LEVELS[level]:
+                ring_wait(s, slot)
+                offset = OFFSETS[slot]
+                direction = -1 if offset > 0 else 1
+                if level < 3 or (level == 3 and direction == (-1 if s == 1 else 1)):
+                    ring_send(s, offset, direction)
+                if s == 2:
+                    block = place.at(0, offset)
+                    start(across_copy(slot, high, block))
+                to_sibling(ref, row, slot)
+        for slot in LEVELS[level - 1]:
+            across_copy(slot, high, place.at(1, OFFSETS[slot])).wait_recv()
+            to_sibling(high, 1, slot)
+    for slot in LEVELS[4]:
+        across_copy(slot, high, place.at(1, OFFSETS[slot])).wait_recv()
+        to_sibling(high, 1, slot)
+    for slot in range(8):
+        for q in range(4):
+            ref, row = (low if q < 2 else high), q % 2
+            block = place.at(row, OFFSETS[slot], 1 - place.c)
+            remote(
+                ref.at[block], ref.at[block], c_send.at[q, slot], c_recv.at[q, slot], sibling
+            ).wait_recv()
+    for copy in sent:
+        copy.wait_send()
+
+
+def scatter_scratch(rows, width):
+    low = split_of(width)
+    high = width - low
+    dma = pltpu.SemaphoreType.DMA
+    half = jnp.bfloat16
+    return [
+        pltpu.VMEM((2, 8, rows, width), half),
+        pltpu.VMEM((8, rows, high), half),
+        pltpu.VMEM((8, rows, high), half),
+        pltpu.VMEM((2, 8, rows, low), half),
+        pltpu.VMEM((2, 8, rows, low), half),
+        pltpu.VMEM((8, rows, high), half),
+        pltpu.VMEM((8, rows, high), half),
+        pltpu.VMEM((2, rows, low), half),
+        dma((2, 8)),
+        dma((2, 8)),
+        dma((9,)),
+        dma((9,)),
+        dma((3, 8)),
+        dma((3, 8)),
+    ]
+
+
+def scatter_sums(place, terms, scratch):
+    (
+        other, high_out, high_in, low_ring_out, low_ring_in, high_ring_out, high_ring_in, last,
+        c_send, c_recv, x_send, x_recv, z_send, z_recv,
+    ) = scratch
+    low = low_ring_out.shape[-1]
+    width = terms.shape[-1]
+    sibling = place.at(0, 0, 1 - place.c)
+    across = place.at(1, 0)
+    sent = []
+    f32 = jnp.float32
+
+    def start(copy):
+        copy.start()
+        sent.append(copy)
+
+    def core_copy(row, slot, over):
+        block = place.at(row, OFFSETS[slot], 1 - place.c)
+        return remote(
+            terms.at[block], other.at[row, over], c_send.at[row, over], c_recv.at[row, over], sibling
+        )
+
+    for level in (4, 3, 2, 1, 0):
+        for slot in LEVELS[level]:
+            for row in (1, 0):
+                start(core_copy(row, slot, MIRROR[slot]))
+
+    have = set()
+
+    def chip_term(row, slot, first, last_col):
+        if (row, slot) not in have:
+            core_copy(row, slot, slot).wait_recv()
+            have.add((row, slot))
+        block = place.at(row, OFFSETS[slot])
+        own = terms[block, :, first:last_col].astype(f32)
+        return own + other[row, slot, :, first:last_col].astype(f32)
+
+    def across_copy(slot):
+        return remote(high_out.at[slot], high_in.at[slot], x_send.at[slot], x_recv.at[slot], across)
+
+    def send_across(level):
+        for slot in LEVELS[level]:
+            high_out[slot] = chip_term(1, slot, low, width).astype(jnp.bfloat16)
+            start(across_copy(slot))
+
+    def ring_bufs(s):
+        if s == 2:
+            return high_ring_out, high_ring_in
+        return low_ring_out.at[s], low_ring_in.at[s]
+
+    def ring_copy(s, slot, landing, target):
+        out, landed = ring_bufs(s)
+        return remote(
+            out.at[slot], landed.at[landing], z_send.at[s, slot], z_recv.at[s, landing], target
+        )
+
+    def landing_of(direction, distance):
+        if distance == 0:
+            return 0 if direction == 1 else 7
+        return OFFSETS.index(direction * distance)
+
+    def local_term(s, slot):
+        if s == 2:
+            value = chip_term(0, slot, low, width)
+            across_copy(slot).wait_recv()
+            return value + high_in[slot].astype(f32)
+        return chip_term(s, slot, 0, low)
+
+    def arrived(s, landing):
+        ring_copy(s, 0, landing, place.at(0, 1)).wait_recv()
+        return ring_bufs(s)[1][landing].astype(f32)
+
+    def ring_level(s, level):
+        long_way = -1 if s == 1 else 1
+        for slot in LEVELS[level]:
+            if level == 4:
+                direction = long_way
+            else:
+                direction = 1 if OFFSETS[slot] > 0 else -1
+            value = local_term(s, slot)
+            if level < 3 or (level == 3 and direction == long_way):
+                value = value + arrived(s, landing_of(direction, level))
+            ring_bufs(s)[0][slot] = value.astype(jnp.bfloat16)
+            start(ring_copy(s, slot, landing_of(direction, level - 1), place.at(0, direction)))
+
+    def ring_end(s):
+        value = local_term(s, 0)
+        for direction in (1, -1):
+            value = value + arrived(s, landing_of(direction, 0))
+        return value
+
+    send_across(4)
+    send_across(3)
+    for level in (4, 3, 2, 1):
+        if level >= 2:
+            send_across(level - 2)
+        for s in (1, 0, 2):
+            ring_level(s, level)
+    last[0] = ring_end(1).astype(jnp.bfloat16)
+    end = remote(last.at[0], last.at[1], x_send.at[8], x_recv.at[8], across)
+    start(end)
+    low_sum = ring_end(0)
+    high_sum = ring_end(2)
+    end.wait_recv()
+    low_sum = low_sum + last[1].astype(f32)
+    for copy in sent:
+        copy.wait_send()
+    return low_sum, high_sum
+
+
+def swap_blocks(place, src, dst, send_sem, recv_sem, count):
+    def copy(j):
+        target = lax.rem(place.t + j, count)
+        return remote(src.at[target], dst.at[place.t], send_sem.at[j], recv_sem.at[j], target)
+
+    def begin(j, carry):
+        copy(j).start()
+        return carry
+
+    def end(j, carry):
+        source = lax.rem(place.t - j + count, count)
+        remote(
+            src.at[source], dst.at[source], send_sem.at[j], recv_sem.at[j], source
+        ).wait_recv()
+        copy(j).wait_send()
+        return carry
+
+    lax.fori_loop(1, count, begin, 0)
+    lax.fori_loop(1, count, end, 0)
+
+
+def normalise(low, high, gain, width):
+    cut = low.shape[-1]
+    total = jnp.sum(low * low, axis=-1, keepdims=True) + jnp.sum(high * high, axis=-1, keepdims=True)
+    scale = lax.rsqrt(total / width + EPSILON)
+    return (
+        (low * scale * gain[:, :cut]).astype(jnp.bfloat16),
+        (high * scale * gain[:, cut:]).astype(jnp.bfloat16),
+    )
+
+
+def vmem():
+    return pl.BlockSpec(memory_space=pltpu.VMEM)
+
+
+def params(identity):
+    return pltpu.CompilerParams(
+        collective_id=identity, has_side_effects=True, vmem_limit_bytes=60 * 2**20
+    )
+
+
+def project_kernel(
+    count, hidden, gain, w_query, w_keyval, out, low, high, projected, landed, *sems
+):
+    place = Place()
+    greet_all(place, count)
+    rows, width = hidden.shape
+    cut = low.shape[-1]
+    values = hidden[...].astype(jnp.float32)
+    first, second = normalise(values[:, :cut], values[:, cut:], gain[...], width)
+    low[place.t] = first
+    high[place.t] = second
+    gather_rows(place, low, high, sems[:6])
+    parts = 4
+    blocks = count // parts
+    for part in range(parts):
+        span = slice(part * blocks, (part + 1) * blocks)
+        low_rows = low[span].reshape(blocks * rows, cut)
+        high_rows = high[span].reshape(blocks * rows, width - cut)
+        start = 0
+        for weights in (w_query, w_keyval):
+            columns = weights.shape[1]
+            value = jnp.dot(low_rows, weights[:cut], preferred_element_type=jnp.float32)
+            value += jnp.dot(high_rows, weights[cut:], preferred_element_type=jnp.float32)
+            projected[span, :, start : start + columns] = value.astype(jnp.bfloat16).reshape(
+                blocks, rows, columns
+            )
+            start += columns
+    landed[place.t] = projected[place.t]
+    swap_blocks(place, projected, landed, sems[6], sems[7], count)
+    out[...] = landed[...]
+
+
+def project(hidden, gain, w_query, w_keyval, count):
+    rows, width = hidden.shape
+    cut = split_of(width)
+    columns = w_query.shape[1] + w_keyval.shape[1]
+    dma = pltpu.SemaphoreType.DMA
+    half = jnp.bfloat16
+    return pl.pallas_call(
+        functools.partial(project_kernel, count),
+        out_shape=jax.ShapeDtypeStruct((count, rows, columns), half),
+        in_specs=[vmem()] * 4,
+        out_specs=vmem(),
+        scratch_shapes=[
+            pltpu.VMEM((count, rows, cut), half),
+            pltpu.VMEM((count, rows, width - cut), half),
+            pltpu.VMEM((count, rows, columns), half),
+            pltpu.VMEM((count, rows, columns), half),
+        ]
+        + gather_sems()
+        + [dma((count,)), dma((count,))],
+        compiler_params=params(0),
+        name="project",
+    )(hidden, gain.reshape(1, width), w_query, w_keyval)
+
+
+def combine_kernel(
+    count, attended, hidden, gain, w_out, middle, low_out, high_out, landed, terms, low, high, *rest
+):
+    place = Place()
+    greet_all(place, count)
+    rows, width = hidden.shape
+    cut = low.shape[-1]
+    swap_send, swap_recv, out_sem = rest[:3]
+    landed[place.t] = attended[place.t]
+    swap_blocks(place, attended, landed, swap_send, swap_recv, count)
+    parts = 4
+    blocks = count // parts
+    for part in range(parts):
+        span = slice(part * blocks, (part + 1) * blocks)
+        heads = landed[span].reshape(blocks * rows, landed.shape[-1])
+        terms[span] = (
+            jnp.dot(heads, w_out[...], preferred_element_type=jnp.float32)
+            .astype(jnp.bfloat16)
+            .reshape(blocks, rows, width)
+        )
+    low_sum, high_sum = scatter_sums(place, terms, rest[9:])
+    values = hidden[...].astype(jnp.float32)
+    low_mid = (values[:, :cut] + low_sum).astype(jnp.bfloat16)
+    high_mid = (values[:, cut:] + high_sum).astype(jnp.bfloat16)
+    middle[:, :cut] = low_mid
+    middle[:, cut:] = high_mid
+    first, second = normalise(
+        low_mid.astype(jnp.float32), high_mid.astype(jnp.float32), gain[...], width
+    )
+    low[place.t] = first
+    high[place.t] = second
+    gather_rows(place, low, high, rest[3:9])
+    copies = [
+        pltpu.make_async_copy(low, low_out, out_sem.at[0]),
+        pltpu.make_async_copy(high, high_out, out_sem.at[1]),
+    ]
+    for copy in copies:
+        copy.start()
+    for copy in copies:
+        copy.wait()
+
+
+def combine(attended, hidden, gain, w_out, count):
+    rows, width = hidden.shape
+    cut = split_of(width)
+    dma = pltpu.SemaphoreType.DMA
+    half = jnp.bfloat16
+    return pl.pallas_call(
+        functools.partial(combine_kernel, count),
+        out_shape=(
+            jax.ShapeDtypeStruct((rows, width), half),
+            jax.ShapeDtypeStruct((count, rows, cut), half),
+            jax.ShapeDtypeStruct((count, rows, width - cut), half),
+        ),
+        in_specs=[vmem()] * 4,
+        out_specs=(vmem(), pl.BlockSpec(memory_space=pl.ANY), pl.BlockSpec(memory_space=pl.ANY)),
+        scratch_shapes=[
+            pltpu.VMEM(attended.shape, half),
+            pltpu.VMEM((count, rows, width), half),
+            pltpu.VMEM((count, rows, cut), half),
+            pltpu.VMEM((count, rows, width - cut), half),
+            dma((count,)),
+            dma((count,)),
+            dma((2,)),
+        ]
+        + gather_sems()
+        + scatter_scratch(rows, width),
+        compiler_params=params(1),
+        name="combine",
+    )(attended, hidden, gain.reshape(1, width), w_out)
+
+
+def finish_kernel(terms, middle, out, *scratch):
+    place = Place()
+    greet(place.neighbours())
+    cut = split_of(middle.shape[-1])
+    low_sum, high_sum = scatter_sums(place, terms, scratch)
+    values = middle[...].astype(jnp.float32)
+    out[:, :cut] = (values[:, :cut] + low_sum).astype(jnp.bfloat16)
+    out[:, cut:] = (values[:, cut:] + high_sum).astype(jnp.bfloat16)
+
+
+def finish_layer(terms, middle):
+    rows, width = middle.shape
+    return pl.pallas_call(
+        finish_kernel,
+        out_shape=jax.ShapeDtypeStruct((rows, width), jnp.bfloat16),
+        in_specs=[vmem()] * 2,
+        out_specs=vmem(),
+        scratch_shapes=scatter_scratch(rows, width),
+        compiler_params=params(2),
+        name="finish_layer",
+    )(terms, middle)
 
 
 def tree_paths(parent_row, depth_limit):
@@ -170,17 +633,10 @@
     devices = lax.axis_size("tp")
     index_me = lax.axis_index("tp")
     rows = hidden.shape[0]
-    normed = rms_norm(hidden, attn_gain)
     local_query = w_query.shape[1]
-    both_weights = jnp.concatenate([w_query, w_keyval], axis=1)
-    projected = jnp.dot(
-        lax.all_gather(normed, "tp", axis=0, tiled=True),
-        both_weights,
-        preferred_element_type=jnp.float32,
-    ).astype(jnp.bfloat16)
-    width = projected.shape[1]
-    gathered_cols = lax.all_to_all(projected, "tp", split_axis=0, concat_axis=1, tiled=True)
-    gathered_cols = gathered_cols.reshape(rows, devices, width)
+    projected = project(hidden, attn_gain, w_query, w_keyval, devices)
+    width = projected.shape[2]
+    gathered_cols = jnp.transpose(projected, (1, 0, 2))
     requests = cache_lens.shape[0]
     draft = parents.shape[1]
     query = gathered_cols[:, :, :local_query].reshape(requests, draft, HEADS, HEAD_DIM)
@@ -194,21 +650,13 @@
     attended, accepted_kv = lax.map(
         per_request, (query, keyval, cache_keys, cache_values, cache_lens, parents, accepted)
     )
-    attended = attended.reshape(rows, HEADS * HEAD_DIM)
-    head_cols = lax.all_to_all(attended, "tp", split_axis=1, concat_axis=0, tiled=True)
-    attn_sum = lax.psum_scatter(
-        jnp.dot(head_cols, w_out, preferred_element_type=jnp.float32),
-        "tp",
-        scatter_dimension=0,
-        tiled=True,
-    )
-    middle = (hidden.astype(jnp.float32) + attn_sum).astype(jnp.bfloat16)
-    moe_in = rms_norm(middle, moe_gain)
-    all_inputs = lax.all_gather(moe_in, "tp", axis=0, tiled=True)
+    attended = jnp.transpose(attended.reshape(rows, devices, local_query), (1, 0, 2))
+    middle, low, high = combine(attended, hidden, moe_gain, w_out, devices)
+    count = devices * rows
+    all_inputs = jnp.concatenate([low, high], axis=2).reshape(count, hidden.shape[1])
     all_weights = gate_weights(all_inputs, w_router, routes)
     units = w_down.shape[0]
     expert = index_me * units // EXPERT_HID
-    count = all_inputs.shape[0]
     capacity = 2 * count * routes.shape[1] // w_router.shape[1]
     slot_rows, slot_index = expert_slots(
         all_inputs, all_weights, routes, expert, w_gate, w_up, w_down, capacity
@@ -218,10 +666,9 @@
         .at[slot_index]
         .add(slot_rows, mode="drop")
     )
-    mixed = lax.psum_scatter(
-        term.astype(jnp.bfloat16), "tp", scatter_dimension=0, tiled=True
-    ).astype(jnp.float32)
-    layer_out = (middle.astype(jnp.float32) + mixed).astype(jnp.bfloat16)
+    layer_out = finish_layer(
+        term.astype(jnp.bfloat16).reshape(devices, rows, all_inputs.shape[1]), middle
+    )
     return (layer_out, accepted_kv)
 
 

time: 526 us -> 246 us (0.47)
  waiting for transfers between devices: 383 us -> 0 us
  Pallas kernels: 0 us -> 146 us
  blocking collectives: 14.8 us -> 0 us
  matrix products: 41.8 us -> 28.1 us
  between operations: 15.5 us -> 2.38 us
  local copies, waits for them, and re-layouts: 29.8 us -> 38.5 us
  starting transfers between devices: 6.85 us -> 0 us
    unnamed x6 -> x0, waiting for transfers between devices: 252 us -> none
    pallas_call x0 -> x3, Pallas kernels: none -> 146 us  [the longest x1 67.7 us: combine(): pl.pallas_call(functools.partial(combine_kernel, count), out_shape=(jax.S...]
    all_gather x2 -> x0, waiting for transfers between devices: 124 us -> none  [the longest x1 63 us: local(): all_inputs = lax.all_gather(moe_in, 'tp', axis=0, tiled=True)]
    all_to_all x1 -> x0, blocking collectives: 14.8 us -> none  [local(): lax.all_to_all(attended, 'tp', split_axis=1, concat_axis=0, tiled=True)]
    dot_general x2 -> x0, matrix products: 10.1 us -> none  [the longest x1 5.93 us: local(): jnp.dot(head_cols, w_out, preferred_element_type=jnp.float32)]
    unnamed x23 -> x33, local copies, waits for them, and re-layouts: 9.63 us -> 16.9 us
    all_to_all x1 -> x0, waiting for transfers between devices: 6.36 us -> none  [local(): lax.all_to_all(projected, 'tp', split_axis=0, concat_axis=1, tiled=True)]
    all_to_all x1 -> x0, starting transfers between devices: 6.28 us -> none  [local(): lax.all_to_all(projected, 'tp', split_axis=0, concat_axis=1, tiled=True)]
  transfers between devices with their start and end apart: 5 -> 0, of which waited for: 5 -> 0; matrix products, arithmetic and copies ran while one was open for 4% -> 0% of each run, Pallas kernels for 0% -> 0%
where the time goes in v1:
time: 246 us; the launch traced here: 245 us
  Pallas kernels  146 us (59%)
  local copies, waits for them, and re-layouts  38.5 us (16%)
  other arithmetic  29.6 us (12%)
  matrix products  28.1 us (11%)
    pallas_call x1, Pallas kernels, combine(): pl.pallas_call(functools.partial(combine_kernel, count), out_shape=(jax.S...  67.7 us
    pallas_call x1, Pallas kernels, project(): pl.pallas_call(functools.partial(project_kernel, count), out_shape=jax.Sh...  49.6 us
    pallas_call x1, Pallas kernels, finish_layer(): pl.pallas_call(finish_kernel, out_shape=jax.ShapeDtypeStruct((rows, width...  29.1 us
    unnamed x33, local copies, waits for them, and re-layouts  16.9 us
    scatter-add x1, other arithmetic, local(): term = jnp.zeros((count, all_inputs.shape[1]), jnp.float32).at[slot_index...  8.74 us
    dot_general x1, matrix products, attend_padded(): jnp.einsum('gqjp,pgd->jgqd', cache_exp.astype(jnp.bfloat16), cache_v, pre...  8.36 us
    dot_general x1, matrix products, attend_padded(): jnp.einsum('jgqd,pgd->gqjp', grouped, cache_k, preferred_element_type=jnp...  8.05 us
    reduce_sum x2, other arithmetic, attend_padded(): total = jnp.sum(draft_exp, axis=-1) + jnp.sum(cache_exp, axis=-1)  6.57 us

profile of v1, /device:TPU:8, one launch (start us, length us, event | category | flops | bytes accessed | tf_op | source)
XLA Modules:
  0.0 245.0 jit_solution(5489310383852575075)
XLA Ops:
  0.6 0.8 compare_select_fusion.3
  1.5 0.6 gather_fusion.2
  2.1 0.7 compare_and_fusion
  2.8 0.6 gather_fusion.3
  3.5 0.6 gather_fusion.4
  4.1 0.6 gather_fusion.5
  4.8 0.6 gather_fusion.6
  5.5 0.6 gather_fusion.7
  6.1 0.6 gather_fusion.8
  6.8 0.6 gather_fusion.9
  8.2 0.6 broadcast_add_fusion
  8.9 2.1 copy.139.w_keyval
  11.0 1.3 reshape.191.gain
  12.3 49.6 %project.1 = bf16[32,24,160]{2,1,0:T(8,128)(2,1)} custom-call(bf16[24,2880]{1,0:T(8,128)(2,1)} %hidden.3, f32[1,2880]{1,0:T(1,128)} %reshape.191.gain, bf16[2880,128]{1,0:T(8,128)(2,1)} %w_query.1, bf16[2880,32]{1,0:T(8,128)(2,1)} %copy.139.w_keyval), custom_call_target="tpu_custom_call" | custom-call | tf_op jit(solution)/shard_map/project/pallas_call | solution.py:375
  61.9 0.9 slice.72
  63.7 0.3 fusion.19
  64.0 0.3 copy.172
  64.2 0.3 copy.171
  64.7 4.0 %copy.151 = bf16[1,2048,512]{1,2,0:T(8,128)(2,1)} copy(bf16[1,2048,512]{2,1,0:T(8,128)(2,1)} %param.23) | data formatting | bytes 4194304 | tf_op args[5]
  68.7 8.1 %bitcast_reduce_fusion = (f32[8,8,24]{1,2,0:T(8,128)S(1)}, f32[8,24,8,2048]{3,2,1,0:T(8,128)}) fusion(pred[2048]{0:T(1024)(128)(4,1)S(1)} %iota_compare_fusion.2, bf16[2048,8,64,1]{0,2,3,1:T(8,128)(2,1)} %bitcast.92, bf16[24,8,8,64]{3,0,2,1:T(8,128)(2,1)S(1)} %pad_maximum_fusion.1), kind=kOutput, calls=%fused_computation.13 | convolution fusion | flops 412088832 | bytes 14884864 | tf_op jit(solution)/shard_map/while/body/eval_jaxpr/jgqd,pgd->gqjp/dot_general | solution.py:556
  76.9 0.2 squeeze.29
  77.6 0.8 fusion.66
  78.5 6.3 %fusion.1 = f32[8,8,24]{1,2,0:T(8,128)S(1)} fusion(f32[8,24,8,2048]{3,2,1,0:T(8,128)} %get-tuple-element.62, f32[8,8,24]{1,2,0:T(8,128)S(1)} %copy.156, pred[2048]{0:T(1024)(128)(4,1)S(1)} %iota_compare_fusion.2), kind=kLoop, calls=%fused_computation.16 | loop fusion | flops 12581376 | bytes 12597248 | tf_op jit(solution)/shard_map/while/body/eval_jaxpr/reduce_sum | solution.py:564
  84.9 0.2 fusion.16
  85.1 4.0 %copy.157 = bf16[1,2048,512]{1,2,0:T(8,128)(2,1)} copy(bf16[1,2048,512]{2,1,0:T(8,128)(2,1)} %param.24) | data formatting | bytes 4194304 | tf_op args[6]
  89.1 8.4 %fusion.3 = f32[8,8,24,64]{3,1,2,0:T(8,128)} fusion(bf16[2048,8,64,1]{0,2,3,1:T(8,128)(2,1)} %bitcast.93, f32[8,24,8,2048]{3,2,1,0:T(8,128)} %get-tuple-element.62, f32[8,8,24]{1,2,0:T(8,128)S(1)} %copy.156, pred[2048]{0:T(1024)(128)(4,1)S(1)} %iota_compare_fusion.2), kind=kOutput, calls=%fused_computation.18 | convolution fusion | flops 415236096 | bytes 15081472 | tf_op jit(solution)/shard_map/while/body/eval_jaxpr/gqjp,pgd->jgqd/dot_general | solution.py:571
  97.6 1.6 fusion.12
  99.5 0.8 copy.191
  100.2 2.3 copy.162.w_out
  102.5 0.6 reshape.197.gain
  103.1 67.7 %combine.1 = (bf16[24,2880]{1,0:T(8,128)(2,1)}, bf16[32,24,1408]{2,1,0:T(8,128)(2,1)}, bf16[32,24,1472]{2,1,0:T(8,128)(2,1)}) custom-call(bf16[32,24,128]{2,1,0:T(8,128)(2,1)} %bitcast.98, bf16[24,2880]{1,0:T(8,128)(2,1)} %hidden.3, f32[1,2880]{1,0:T(1,128)} %reshape.197.gain, bf16[128,2880]{1,0:T(8,128)(2,1)} %copy.162.w_out), custom_call_target="tpu_custom_call" | custom-call | tf_op jit(solution)/shard_map/combine/pallas_call | solution.py:440
  170.8 2.7 %pad_maximum_fusion = bf16[32,24,2880]{2,1,0:T(8,128)(2,1)S(1)} fusion(bf16[32,24,1472]{2,1,0:T(8,128)(2,1)} %get-tuple-element.27, bf16[32,24,1408]{2,1,0:T(8,128)(2,1)} %get-tuple-element.26), kind=kLoop, calls=%fused_computation.20 | loop fusion | flops 8847360 | bytes 8847360 | tf_op jit(solution)/shard_map/concatenate | solution.py:656
  173.5 2.0 copy-done.1
  175.6 1.3 fusion.68
  177.1 0.3 reduce-window.9
  177.8 3.6 %scatter_custom_fusion = s32[192]{0:T(256)S(1)} fusion(s32[768]{0:T(1024)S(1)} %fusion.52, s32[768]{0:T(1024)S(1)} %iota.71, s32[]{:T(128)} %constant.28.clone.1), kind=kCustom, calls=%fused_computation.113 | custom fusion | bytes 772 | tf_op jit(solution)/shard_map/scatter | solution.py:597
  181.4 0.6 compare_select_fusion.1
  182.0 0.6 copy-done.10
  182.5 5.3 %gather_fusion = bf16[192,2880]{1,0:T(8,128)(2,1)S(1)} fusion(bf16[768,2880]{1,0:T(8,128)(2,1)} %bitcast.90, s32[1024]{0:T(1024)S(1)} %pad_clamp_fusion), kind=kCustom, calls=%fused_computation.8 | custom fusion | bytes 2212608 | tf_op jit(solution)/shard_map/gather | solution.py:600
  187.9 2.5 %fusion.67 = f32[192,360]{1,0:T(8,128)S(1)} fusion(bf16[192,2880]{1,0:T(8,128)(2,1)S(1)} %gather_fusion, bf16[360,2880]{1,0:T(8,128)(2,1)} %param.31), kind=kOutput, calls=%fused_computation.125 | convolution fusion | flops 398131200 | bytes 3456000 | tf_op jit(solution)/shard_map/dot_general | solution.py:601
  190.4 1.9 gather_fusion.1
  192.3 0.7 compare_select_fusion.4
  193.0 4.8 %convolution_multiply_fusion = f32[192,2880]{1,0:T(8,128)} fusion(bf16[360,2880]{1,0:T(8,128)(2,1)S(1)} %copy-done, bf16[192,2880]{1,0:T(8,128)(2,1)S(1)} %gather_fusion, bf16[360,2880]{1,0:T(8,128)(2,1)} %param.32, f32[192]{0:T(256)S(1)} %compare_select_fusion.4, f32[192,360]{1,0:T(8,128)S(1)} %fusion.67), kind=kOutput, calls=%fused_computation.23 | convolution fusion | flops 797368320 | bytes 7742208 | tf_op jit(solution)/shard_map/dot_general | solution.py:610
  197.8 8.7 %scatter_custom_fusion.1 = f32[768,2880]{1,0:T(8,128)} fusion(s32[192]{0:T(256)} %get-tuple-element.54, f32[192,2880]{1,0:T(8,128)} %convolution_multiply_fusion, f32[]{:T(128)} %constant.27.clone.1), kind=kCustom, calls=%fused_computation.21 | custom fusion | flops 552960 | bytes 8847872 | tf_op jit(solution)/shard_map/scatter-add | solution.py:667
  206.5 6.2 %convert_element_type.101 = bf16[768,2880]{1,0:T(8,128)(2,1)} convert(f32[768,2880]{1,0:T(8,128)} %scatter_custom_fusion.1) | non-fusion elementwise | flops 2211840 | bytes 13271040 | tf_op jit(solution)/shard_map/convert_element_type | solution.py:670
  212.7 29.1 %finish_layer.1 = bf16[24,2880]{1,0:T(8,128)(2,1)} custom-call(bf16[32,24,2880]{2,1,0:T(8,128)(2,1)} %bitcast.91, bf16[24,2880]{1,0:T(8,128)(2,1)} %get-tuple-element.28.middle), custom_call_target="tpu_custom_call" | custom-call | tf_op jit(solution)/shard_map/finish_layer/pallas_call | solution.py:477
  242.6 0.7 fusion.15
  243.4 1.6 copy.195
  (75 shorter events, 3.7 us)
Async XLA Ops:
  0.6 192.3 %copy-start = (bf16[360,2880]{1,0:T(8,128)(2,1)S(1)}, bf16[360,2880]{1,0:T(8,128)(2,1)}, u32[]{:S(2)}) copy-start(bf16[360,2880]{1,0:T(8,128)(2,1)} %param.33) | copy-start | bytes 6220804
  68.7 8.1 %copy-start.2 = (bf16[32,24,160]{2,1,0:T(8,128)(2,1)S(1)}, bf16[32,24,160]{2,1,0:T(8,128)(2,1)}, u32[]{:S(2)}) copy-start(bf16[32,24,160]{2,1,0:T(8,128)(2,1)} %project.1) | copy-start | bytes 737284
  77.2 20.3 %copy-start.6 = (bf16[24,512]{1,0:T(8,128)(2,1)}, bf16[24,512]{1,0:T(8,128)(2,1)S(1)}, u32[]{:S(2)}) copy-start(bf16[24,512]{1,0:T(8,128)(2,1)S(1)} %get-tuple-element.49) | copy-start | bytes 73732
  77.5 7.3 %copy-start.3 = (bf16[24,8,64]{2,0,1:T(8,128)(2,1)}, bf16[24,8,64]{2,0,1:T(8,128)(2,1)S(1)}, u32[]{:S(2)}) copy-start(bf16[24,8,64]{2,0,1:T(8,128)(2,1)S(1)} %maximum_convert_fusion) | copy-start | bytes 73732
  97.6 4.9 %copy-start.9 = (f32[2880]{0:T(1024)S(1)}, f32[2880]{0:T(1024)}, u32[]{:S(2)}) copy-start(f32[2880]{0:T(1024)} %param.28) | copy-start | bytes 34564
  170.8 4.8 %copy-start.5 = (bf16[2880,32]{0,1:T(8,128)(2,1)S(1)}, bf16[2880,32]{0,1:T(8,128)(2,1)}, u32[]{:S(2)}) copy-start(bf16[2880,32]{0,1:T(8,128)(2,1)} %param.29) | copy-start | bytes 552964
  173.5 2.1 copy-start.1
  173.5 3.4 %copy-start.8 = (s32[768,4]{0,1:T(4,128)S(1)}, s32[768,4]{0,1:T(4,128)}, u32[]{:S(2)}) copy-start(s32[768,4]{0,1:T(4,128)} %param.30) | copy-start | bytes 36868
  181.4 0.6 copy-start.11
  182.0 0.6 copy-start.10
  212.7 29.1 %copy-start.4 = (bf16[24,8,64]{2,0,1:T(8,128)(2,1)S(1)}, bf16[24,8,64]{2,0,1:T(8,128)(2,1)}, u32[]{:S(2)}) copy-start(bf16[24,8,64]{2,0,1:T(8,128)(2,1)} %copy-done.3) | copy-start | bytes 73732
  212.7 29.9 %copy-start.7 = (bf16[24,512]{1,0:T(8,128)(2,1)S(1)}, bf16[24,512]{1,0:T(8,128)(2,1)}, u32[]{:S(2)}) copy-start(bf16[24,512]{1,0:T(8,128)(2,1)} %copy-done.6) | copy-start | bytes 73732
  212.7 29.9 %copy-start.12 = (s32[24]{0:T(128)S(1)}, s32[24]{0:T(128)}, u32[]{:S(2)}) copy-start(s32[24]{0:T(128)} %get-tuple-element.57) | copy-start | bytes 292

commit v2 on v1

v2 whole, which is shorter than its diff:
```python
import functools
import math

import jax
import jax.numpy as jnp
from jax import lax
from jax.experimental import pallas as pl
from jax.experimental.pallas import tpu as pltpu
from jax.sharding import PartitionSpec as P

HEADS = 64
HEAD_DIM = 64
EXPERT_HID = 2880
DEPTH = 8


THETA = 150000.0
SWIGLU_ALPHA = 1.702
EPSILON = 1e-05

MESH = pl.DeviceIdType.MESH
RING = 8
OFFSETS = (0, 1, -1, 2, -2, 3, -3, 4)
MIRROR = (0, 2, 1, 4, 3, 6, 5, 7)
LEVELS = ((0,), (1, 2), (3, 4), (5, 6), (7,))


def split_of(width):
    return (width // 2) // 128 * 128


class Place:
    def __init__(self):
        self.t = lax.axis_index("tp")
        self.c = lax.rem(self.t, 2)
        self.z = lax.rem(self.t // 2, RING)
        self.x = self.t // (2 * RING)
        self.forward = 1 - 2 * self.c

    def at(self, row, offset, core=None):
        z = lax.rem(self.z + self.forward * offset + 2 * RING, RING)
        x = self.x if row == 0 else 1 - self.x
        return (x * RING + z) * 2 + (self.c if core is None else core)

    def blocks(self, level):
        return [
            self.at(row, OFFSETS[slot], core)
            for slot in LEVELS[level]
            for row in (0, 1)
            for core in (self.c, 1 - self.c)
        ]


def greet_all(place, count):
    barrier = pltpu.get_barrier_semaphore()

    def one(j, carry):
        pl.semaphore_signal(
            barrier, inc=1, device_id={"tp": lax.rem(place.t + j, count)}, device_id_type=MESH
        )
        return carry

    lax.fori_loop(1, count, one, 0)
    pl.semaphore_wait(barrier, count - 1)


def remote(src, dst, send_sem, recv_sem, target):
    return pltpu.make_async_remote_copy(
        src_ref=src,
        dst_ref=dst,
        send_sem=send_sem,
        recv_sem=recv_sem,
        device_id={"tp": target},
        device_id_type=MESH,
    )


def gather_sems():
    dma = pltpu.SemaphoreType.DMA
    return [dma((3, 8)), dma((3, 8)), dma((9,)), dma((9,)), dma((4, 8)), dma((4, 8))]


def gather_rows(place, low, high, sems, work):
    z_send, z_recv, x_send, x_recv, c_send, c_recv = sems
    streams = ((low, 0), (low, 1), (high, 0))
    sibling = place.at(0, 0, 1 - place.c)
    across = place.at(1, 0)
    sent = []

    def start(copy):
        copy.start()
        sent.append(copy)

    def ring_copy(s, slot, block, target):
        ref = streams[s][0]
        return remote(ref.at[block], ref.at[block], z_send.at[s, slot], z_recv.at[s, slot], target)

    def ring_send(s, offset, direction):
        landed = offset - direction
        slot = OFFSETS.index(4 if landed == -4 else landed)
        block = place.at(streams[s][1], offset)
        start(ring_copy(s, slot, block, place.at(0, direction)))

    def ring_wait(s, slot):
        block = place.at(streams[s][1], OFFSETS[slot])
        ring_copy(s, slot, block, place.at(0, 1)).wait_recv()

    def across_copy(slot, ref, block):
        return remote(ref.at[block], ref.at[block], x_send.at[slot], x_recv.at[slot], across)

    def to_sibling(ref, row, slot):
        q = (0 if ref is low else 2) + row
        block = place.at(row, OFFSETS[slot])
        over = MIRROR[slot]
        start(
            remote(ref.at[block], ref.at[block], c_send.at[q, over], c_recv.at[q, over], sibling)
        )

    def settle(level):
        for slot in LEVELS[level]:
            across_copy(slot, high, place.at(1, OFFSETS[slot])).wait_recv()
            to_sibling(high, 1, slot)
        for slot in LEVELS[level]:
            for q in range(4):
                ref, row = (low if q < 2 else high), q % 2
                block = place.at(row, OFFSETS[slot], 1 - place.c)
                remote(
                    ref.at[block], ref.at[block], c_send.at[q, slot], c_recv.at[q, slot], sibling
                ).wait_recv()
        work(level)

    mine = place.t
    start(across_copy(8, low, mine))
    for s in (0, 2):
        for direction in (1, -1):
            ring_send(s, 0, direction)
    start(across_copy(0, high, mine))
    to_sibling(low, 0, 0)
    to_sibling(high, 0, 0)
    across_copy(8, low, across).wait_recv()
    for direction in (1, -1):
        ring_send(1, 0, direction)
    to_sibling(low, 1, 0)
    for level in range(1, 5):
        for s in (0, 2, 1):
            ref, row = streams[s]
            for slot in LEVELS[level]:
                ring_wait(s, slot)
                offset = OFFSETS[slot]
                direction = -1 if offset > 0 else 1
                if level < 3 or (level == 3 and direction == (-1 if s == 1 else 1)):
                    ring_send(s, offset, direction)
                if s == 2:
                    block = place.at(0, offset)
                    start(across_copy(slot, high, block))
                to_sibling(ref, row, slot)
        settle(level - 1)
    settle(4)
    for copy in sent:
        copy.wait_send()


def scatter_scratch(rows, width):
    low = split_of(width)
    high = width - low
    dma = pltpu.SemaphoreType.DMA
    half = jnp.bfloat16
    return [
        pltpu.VMEM((2, 8, rows, width), half),
        pltpu.VMEM((8, rows, high), half),
        pltpu.VMEM((8, rows, high), half),
        pltpu.VMEM((2, 8, rows, low), half),
        pltpu.VMEM((2, 8, rows, low), half),
        pltpu.VMEM((8, rows, high), half),
        pltpu.VMEM((8, rows, high), half),
        pltpu.VMEM((2, rows, low), half),
        dma((2, 8)),
        dma((2, 8)),
        dma((9,)),
        dma((9,)),
        dma((3, 8)),
        dma((3, 8)),
    ]


def core_term(place, terms, scratch, row, slot, over):
    other, c_send, c_recv = scratch[0], scratch[8], scratch[9]
    sibling = place.at(0, 0, 1 - place.c)
    block = place.at(row, OFFSETS[slot], 1 - place.c)
    return remote(
        terms.at[block], other.at[row, over], c_send.at[row, over], c_recv.at[row, over], sibling
    )


def core_terms(place, terms, scratch, level):
    copies = [
        core_term(place, terms, scratch, row, slot, MIRROR[slot])
        for slot in LEVELS[level]
        for row in (1, 0)
    ]
    for copy in copies:
        copy.start()
    return copies


def scatter_sums(place, terms, scratch, core_sent):
    (
        other, high_out, high_in, low_ring_out, low_ring_in, high_ring_out, high_ring_in, last,
        _, _, x_send, x_recv, z_send, z_recv,
    ) = scratch
    low = low_ring_out.shape[-1]
    width = terms.shape[-1]
    across = place.at(1, 0)
    sent = []
    f32 = jnp.float32

    def start(copy):
        copy.start()
        sent.append(copy)

    def core_copy(row, slot, over):
        return core_term(place, terms, scratch, row, slot, over)

    sent.extend(core_sent)
    have = set()

    def chip_term(row, slot, first, last_col):
        if (row, slot) not in have:
            core_copy(row, slot, slot).wait_recv()
            have.add((row, slot))
        block = place.at(row, OFFSETS[slot])
        own = terms[block, :, first:last_col].astype(f32)
        return own + other[row, slot, :, first:last_col].astype(f32)

    def across_copy(slot):
        return remote(high_out.at[slot], high_in.at[slot], x_send.at[slot], x_recv.at[slot], across)

    def send_across(level):
        for slot in LEVELS[level]:
            high_out[slot] = chip_term(1, slot, low, width).astype(jnp.bfloat16)
            start(across_copy(slot))

    def ring_bufs(s):
        if s == 2:
            return high_ring_out, high_ring_in
        return low_ring_out.at[s], low_ring_in.at[s]

    def ring_copy(s, slot, landing, target):
        out, landed = ring_bufs(s)
        return remote(
            out.at[slot], landed.at[landing], z_send.at[s, slot], z_recv.at[s, landing], target
        )

    def landing_of(direction, distance):
        if distance == 0:
            return 0 if direction == 1 else 7
        return OFFSETS.index(direction * distance)

    def local_term(s, slot):
        if s == 2:
            value = chip_term(0, slot, low, width)
            across_copy(slot).wait_recv()
            return value + high_in[slot].astype(f32)
        return chip_term(s, slot, 0, low)

    def arrived(s, landing):
        ring_copy(s, 0, landing, place.at(0, 1)).wait_recv()
        return ring_bufs(s)[1][landing].astype(f32)

    def ring_level(s, level):
        long_way = -1 if s == 1 else 1
        for slot in LEVELS[level]:
            if level == 4:
                direction = long_way
            else:
                direction = 1 if OFFSETS[slot] > 0 else -1
            value = local_term(s, slot)
            if level < 3 or (level == 3 and direction == long_way):
                value = value + arrived(s, landing_of(direction, level))
            ring_bufs(s)[0][slot] = value.astype(jnp.bfloat16)
            start(ring_copy(s, slot, landing_of(direction, level - 1), place.at(0, direction)))

    def ring_end(s):
        value = local_term(s, 0)
        for direction in (1, -1):
            value = value + arrived(s, landing_of(direction, 0))
        return value

    send_across(4)
    send_across(3)
    for level in (4, 3, 2, 1):
        if level >= 2:
            send_across(level - 2)
        for s in (1, 0, 2):
            ring_level(s, level)
    last[0] = ring_end(1).astype(jnp.bfloat16)
    end = remote(last.at[0], last.at[1], x_send.at[8], x_recv.at[8], across)
    start(end)
    low_sum = ring_end(0)
    high_sum = ring_end(2)
    end.wait_recv()
    low_sum = low_sum + last[1].astype(f32)
    for copy in sent:
        copy.wait_send()
    return low_sum, high_sum


def swap_send(place, src, dst, send_sem, recv_sem, level):
    copies = []
    for block in place.blocks(level):
        if level == 0 and not copies:
            copies.append(None)
            continue
        copy = remote(
            src.at[block], dst.at[place.t], send_sem.at[block], recv_sem.at[place.t], block
        )
        copy.start()
        copies.append(copy)
    return [copy for copy in copies if copy is not None]


def swap_wait(place, src, dst, send_sem, recv_sem, level):
    for i, block in enumerate(place.blocks(level)):
        if level == 0 and i == 0:
            continue
        remote(
            src.at[block], dst.at[block], send_sem.at[block], recv_sem.at[block], block
        ).wait_recv()


def normalise(low, high, gain, width):
    cut = low.shape[-1]
    total = jnp.sum(low * low, axis=-1, keepdims=True) + jnp.sum(high * high, axis=-1, keepdims=True)
    scale = lax.rsqrt(total / width + EPSILON)
    return (
        (low * scale * gain[:, :cut]).astype(jnp.bfloat16),
        (high * scale * gain[:, cut:]).astype(jnp.bfloat16),
    )


def vmem():
    return pl.BlockSpec(memory_space=pltpu.VMEM)


def in_place():
    return pl.BlockSpec(memory_space=pl.ANY)


def params(identity):
    return pltpu.CompilerParams(
        collective_id=identity, has_side_effects=True, vmem_limit_bytes=60 * 2**20
    )


def dot_rows(a, b):
    return lax.dot_general(a, b, (((1,), (1,)), ((), ())), preferred_element_type=jnp.float32)


def stage(buffer, ref, blocks):
    for i, block in enumerate(blocks):
        buffer[i] = ref[block]
    value = buffer[: len(blocks)]
    return value.reshape(len(blocks) * value.shape[1], value.shape[2])


def project_kernel(
    count, hidden, gain, w_query, w_keyval, out,
    low, high, projected, landed, stage_low, stage_high, swap_out, swap_in, *sems
):
    place = Place()
    greet_all(place, count)
    rows, width = hidden.shape
    cut = low.shape[-1]
    values = hidden[...].astype(jnp.float32)
    first, second = normalise(values[:, :cut], values[:, cut:], gain[...], width)
    low[place.t] = first
    high[place.t] = second
    sent = []
    split = w_query.shape[1]

    def work(level):
        blocks = place.blocks(level)
        low_rows = stage(stage_low, low, blocks)
        high_rows = stage(stage_high, high, blocks)
        query = jnp.dot(low_rows, w_query[:cut], preferred_element_type=jnp.float32)
        query += jnp.dot(high_rows, w_query[cut:], preferred_element_type=jnp.float32)
        keyval = dot_rows(low_rows, w_keyval[:, :cut]) + dot_rows(high_rows, w_keyval[:, cut:])
        query = query.astype(jnp.bfloat16).reshape(len(blocks), rows, split)
        keyval = keyval.astype(jnp.bfloat16).reshape(len(blocks), rows, w_keyval.shape[0])
        for i, block in enumerate(blocks):
            projected[block, :, :split] = query[i]
            projected[block, :, split:] = keyval[i]
        sent.extend(swap_send(place, projected, landed, swap_out, swap_in, level))

    gather_rows(place, low, high, sems, work)
    landed[place.t] = projected[place.t]
    for level in range(5):
        swap_wait(place, projected, landed, swap_out, swap_in, level)
    for copy in sent:
        copy.wait_send()
    out[...] = landed[...]


def project(hidden, gain, w_query, w_keyval, count):
    rows, width = hidden.shape
    cut = split_of(width)
    columns = w_query.shape[1] + w_keyval.shape[0]
    dma = pltpu.SemaphoreType.DMA
    half = jnp.bfloat16
    return pl.pallas_call(
        functools.partial(project_kernel, count),
        out_shape=jax.ShapeDtypeStruct((count, rows, columns), half),
        in_specs=[vmem()] * 4,
        out_specs=vmem(),
        scratch_shapes=[
            pltpu.VMEM((count, rows, cut), half),
            pltpu.VMEM((count, rows, width - cut), half),
            pltpu.VMEM((count, rows, columns), half),
            pltpu.VMEM((count, rows, columns), half),
            pltpu.VMEM((8, rows, cut), half),
            pltpu.VMEM((8, rows, width - cut), half),
            dma((count,)),
            dma((count,)),
        ]
        + gather_sems(),
        compiler_params=params(0),
        name="project",
    )(hidden, gain.reshape(1, width), w_query, w_keyval)


def attend_kernel(
    lens, leaf, parents, blocks, keys, values, out, accepted, key_tiles, value_tiles, scores, sems
):
    f32 = jnp.float32
    half = jnp.bfloat16
    pairs = key_tiles.shape[0]
    draft = parents.shape[1]
    chunks, rows, span = scores.shape

    def loads(pair):
        columns = slice(pair * 128, (pair + 1) * 128)
        return (
            pltpu.make_async_copy(keys.at[0, :, columns], key_tiles.at[pair], sems.at[0, pair]),
            pltpu.make_async_copy(values.at[0, :, columns], value_tiles.at[pair], sems.at[1, pair]),
        )

    for pair in range(pairs):
        for copy in loads(pair):
            copy.start()
    length = lens[0]
    k_of = lax.broadcasted_iota(jnp.int32, (draft, draft), 0)
    j_of = lax.broadcasted_iota(jnp.int32, (draft, draft), 1)
    eye = (k_of == j_of).astype(half)
    is_parent = k_of == jnp.broadcast_to(parents[...], (draft, draft))
    paths = jnp.where(is_parent | (k_of == j_of), 1.0, 0.0)
    for _ in range(3):
        paths = jnp.dot(paths.astype(half), paths.astype(half), preferred_element_type=f32)
        paths = jnp.minimum(paths, 1.0)
    ancestry = lax.dot_general(
        paths.astype(half), eye, (((0,), (0,)), ((), ())), preferred_element_type=f32
    )
    depth_row = jnp.sum(paths, axis=0, keepdims=True) - 1.0
    depth = jnp.sum(ancestry, axis=1, keepdims=True) - 1.0
    positions = length.astype(f32) + depth
    lane = lax.broadcasted_iota(jnp.int32, (draft, 128), 1)
    first_half = lane % 64 < 32
    low_lanes = lane < 64
    inverse = jnp.exp((lane % 32).astype(f32) * (-2.0 * math.log(THETA) / HEAD_DIM))
    angles = positions * inverse
    cosine = jnp.cos(angles)
    sine = jnp.sin(angles)
    signed = jnp.where(first_half, -sine, sine)

    def rotated(value):
        partner = jnp.where(first_half, pltpu.roll(value, 96, 1), pltpu.roll(value, 32, 1))
        return (value * cosine + partner * signed).astype(half)

    def columns_of(first):
        return jnp.concatenate([blocks[first + q, :, 128:160].astype(f32) for q in range(4)], axis=1)

    on_path = jnp.sum(jnp.where(k_of == leaf[0], ancestry, 0.0), axis=0, keepdims=True)
    level = lax.broadcasted_iota(jnp.int32, (DEPTH, draft), 0).astype(f32)
    selector = jnp.where((on_path > 0.5) & (depth_row == level), 1.0, 0.0).astype(half)
    allowed = jnp.concatenate([ancestry] * 16, axis=0) > 0.5
    scale = 1.0 / math.sqrt(HEAD_DIM)

    for pair in range(pairs):
        new_keys = rotated(columns_of(4 * pair))
        new_values = columns_of(16 + 4 * pair).astype(half)
        columns = slice(pair * 128, (pair + 1) * 128)
        accepted[0, :, columns] = jnp.dot(selector, new_keys, preferred_element_type=f32).astype(half)
        columns = slice((4 + pair) * 128, (5 + pair) * 128)
        accepted[0, :, columns] = jnp.dot(
            selector, new_values, preferred_element_type=f32
        ).astype(half)
        lhs = []
        for i in range(8):
            turned = rotated(blocks[8 * pair + i, :, :128].astype(f32)).astype(f32) * scale
            swapped = pltpu.roll(turned, 64, 1)
            if i < 4:
                lhs.append(jnp.where(low_lanes, turned, 0.0))
                lhs.append(jnp.where(low_lanes, swapped, 0.0))
            else:
                lhs.append(jnp.where(low_lanes, 0.0, swapped))
                lhs.append(jnp.where(low_lanes, 0.0, turned))
        lhs = jnp.concatenate(lhs, axis=0).astype(half)
        draft_scores = jnp.where(allowed, dot_rows(lhs, new_keys), -jnp.inf)
        top = jnp.max(draft_scores, axis=1, keepdims=True)
        key_copy, value_copy = loads(pair)
        key_copy.wait()
        for n in range(chunks):
            part = dot_rows(lhs, key_tiles[pair, n * span : (n + 1) * span, :])
            slot = n * span + lax.broadcasted_iota(jnp.int32, (1, span), 1)
            part = jnp.where(slot < length, part, -jnp.inf)
            scores[n] = part
            top = jnp.maximum(top, jnp.max(part, axis=1, keepdims=True))
        weights = jnp.exp(draft_scores - top)
        total = jnp.sum(weights, axis=1, keepdims=True)
        weighted = jnp.dot(weights.astype(half), new_values, preferred_element_type=f32)
        value_copy.wait()
        for n in range(chunks):
            weights = jnp.exp(scores[n] - top)
            total = total + jnp.sum(weights, axis=1, keepdims=True)
            weighted = weighted + jnp.dot(
                weights.astype(half),
                value_tiles[pair, n * span : (n + 1) * span, :],
                preferred_element_type=f32,
            )
        result = weighted / total
        for i in range(8):
            even = result[2 * i * draft : (2 * i + 1) * draft]
            odd = result[(2 * i + 1) * draft : (2 * i + 2) * draft]
            if i < 4:
                both = jnp.where(low_lanes, even, pltpu.roll(odd, 64, 1))
            else:
                both = jnp.where(low_lanes, pltpu.roll(even, 64, 1), odd)
            out[8 * pair + i] = both.astype(half)


def attend(lens, leaf, parents, blocks, keys, values):
    count, draft, _ = blocks.shape
    _, slots, kv_width = keys.shape
    pairs = kv_width // 128
    chunks = 4
    half = jnp.bfloat16
    smem = pl.BlockSpec(memory_space=pltpu.SMEM)
    return pl.pallas_call(
        attend_kernel,
        out_shape=(
            jax.ShapeDtypeStruct((count, draft, 128), half),
            jax.ShapeDtypeStruct((1, DEPTH, 2 * kv_width), half),
        ),
        in_specs=[smem, smem, vmem(), vmem(), in_place(), in_place()],
        out_specs=(vmem(), vmem()),
        scratch_shapes=[
            pltpu.VMEM((pairs, slots, 128), half),
            pltpu.VMEM((pairs, slots, 128), half),
            pltpu.VMEM((chunks, 16 * draft, slots // chunks), jnp.float32),
            pltpu.SemaphoreType.DMA((2, pairs)),
        ],
        compiler_params=pltpu.CompilerParams(vmem_limit_bytes=60 * 2**20),
        name="attend",
    )(lens, leaf, parents, blocks, keys, values)


def layer_kernel(
    count, attended, hidden, gain, routes, w_router, w_out_hbm, w_gate_hbm, w_up_hbm, w_down_hbm, out,
    w_out, w_gate, w_up, w_down, weight_sems, landed, stage_heads, terms, low, high,
    stage_low, stage_high, route_cols, stage_routes, swap_out, swap_in, *rest
):
    place = Place()
    f32 = jnp.float32
    half = jnp.bfloat16
    weights = [
        pltpu.make_async_copy(source, target, weight_sems.at[i])
        for i, (source, target) in enumerate(
            ((w_out_hbm, w_out), (w_gate_hbm, w_gate), (w_up_hbm, w_up), (w_down_hbm, w_down))
        )
    ]
    for copy in weights:
        copy.start()
    greet_all(place, count)
    rows, width = hidden.shape
    cut = low.shape[-1]
    gather_scratch, first_scratch, second_scratch = rest[:6], rest[6:20], rest[20:]
    swaps = (place, attended, landed, swap_out, swap_in)
    sent = []
    for level in (4, 3, 2, 1, 0):
        sent.extend(swap_send(*swaps, level))
    landed[place.t] = attended[place.t]
    top = routes.shape[0]
    pick = (
        lax.broadcasted_iota(jnp.int32, (top, top), 0)
        == lax.broadcasted_iota(jnp.int32, (top, top), 1)
    ).astype(half)
    route_cols[...] = lax.dot_general(
        routes[...].astype(f32).astype(half), pick, (((0,), (0,)), ((), ())), preferred_element_type=f32
    ).reshape(count, rows, top)
    weights[0].wait()
    core_sent = []
    for level in (4, 3, 2, 1, 0):
        swap_wait(*swaps, level)
        blocks = place.blocks(level)
        heads = stage(stage_heads, landed, blocks)
        product = dot_rows(heads, w_out[...]).astype(half).reshape(len(blocks), rows, width)
        for i, block in enumerate(blocks):
            terms[block] = product[i]
        core_sent.extend(core_terms(place, terms, first_scratch, level))
    low_sum, high_sum = scatter_sums(place, terms, first_scratch, core_sent)
    for copy in sent:
        copy.wait_send()
    values = hidden[...].astype(f32)
    low_mid = (values[:, :cut] + low_sum).astype(half)
    high_mid = (values[:, cut:] + high_sum).astype(half)
    first, second = normalise(low_mid.astype(f32), high_mid.astype(f32), gain[...], width)
    low[place.t] = first
    high[place.t] = second
    for copy in weights[1:]:
        copy.wait()
    units = w_down.shape[0]
    expert = (place.t * units // EXPERT_HID).astype(f32)
    core_sent = []

    def experts(level):
        blocks = place.blocks(level)
        low_rows = stage(stage_low, low, blocks)
        high_rows = stage(stage_high, high, blocks)
        named = stage(stage_routes, route_cols, blocks)
        every = len(blocks) * rows

        def along(matrix):
            return dot_rows(low_rows, matrix[:, :cut]) + dot_rows(high_rows, matrix[:, cut:])

        logits = along(w_router)
        index = lax.broadcasted_iota(jnp.int32, (every, w_router.shape[0]), 1).astype(f32)
        names = [named[:, i : i + 1] for i in range(top)]
        picked = [
            jnp.sum(jnp.where(name == index, logits, 0.0), axis=1, keepdims=True) for name in names
        ]
        peak = functools.reduce(jnp.maximum, picked)
        shares = [jnp.exp(value - peak) for value in picked]
        total = functools.reduce(jnp.add, shares)
        gate_of = jnp.zeros_like(total)
        hit = jnp.zeros_like(total)
        for name, share in zip(names, shares):
            weight = (share / total).astype(half).astype(f32)
            gate_of = gate_of + jnp.where(name == expert, weight, 0.0)
            hit = hit + jnp.where(name == expert, 1.0, 0.0)
        gate = along(w_gate)
        up = along(w_up)
        active = (gate * jax.nn.sigmoid(SWIGLU_ALPHA * gate) * (up + 1.0)).astype(half)
        result = jnp.dot(active, w_down[...], preferred_element_type=f32)
        result = jnp.where(hit > 0.5, result * gate_of, 0.0).astype(half)
        result = result.reshape(len(blocks), rows, width)
        for i, block in enumerate(blocks):
            terms[block] = result[i]
        core_sent.extend(core_terms(place, terms, second_scratch, level))

    gather_rows(place, low, high, gather_scratch, experts)
    low_sum, high_sum = scatter_sums(place, terms, second_scratch, core_sent)
    out[:, :cut] = low_mid.astype(f32) + low_sum
    out[:, cut:] = high_mid.astype(f32) + high_sum


def layer(attended, hidden, gain, routes, w_router, w_out, w_gate, w_up, w_down):
    rows, width = hidden.shape
    count = attended.shape[0]
    cut = split_of(width)
    top = routes.shape[0]
    dma = pltpu.SemaphoreType.DMA
    half = jnp.bfloat16
    return pl.pallas_call(
        functools.partial(layer_kernel, count),
        out_shape=jax.ShapeDtypeStruct((rows, width), jnp.float32),
        in_specs=[vmem()] * 5 + [in_place()] * 4,
        out_specs=vmem(),
        scratch_shapes=[
            pltpu.VMEM(w_out.shape, half),
            pltpu.VMEM(w_gate.shape, half),
            pltpu.VMEM(w_up.shape, half),
            pltpu.VMEM(w_down.shape, half),
            dma((4,)),
            pltpu.VMEM(attended.shape, half),
            pltpu.VMEM((8, rows, attended.shape[2]), half),
            pltpu.VMEM((count, rows, width), half),
            pltpu.VMEM((count, rows, cut), half),
            pltpu.VMEM((count, rows, width - cut), half),
            pltpu.VMEM((8, rows, cut), half),
            pltpu.VMEM((8, rows, width - cut), half),
            pltpu.VMEM((count, rows, top), jnp.float32),
            pltpu.VMEM((8, rows, top), jnp.float32),
            dma((count,)),
            dma((count,)),
        ]
        + gather_sems()
        + scatter_scratch(rows, width)
        + scatter_scratch(rows, width),
        compiler_params=params(1),
        name="layer",
    )(attended, hidden, gain.reshape(1, width), routes, w_router, w_out, w_gate, w_up, w_down)


def local(
    hidden,
    attn_gain,
    w_query,
    w_keyval,
    w_out,
    cache_keys,
    cache_values,
    cache_lens,
    parents,
    accepted,
    moe_gain,
    w_router,
    routes,
    w_gate,
    w_up,
    w_down,
):
    devices = lax.axis_size("tp")
    projected = project(hidden, attn_gain, w_query, w_keyval.T, devices)
    attended, accepted_kv = attend(
        cache_lens, accepted, parents, projected, cache_keys, cache_values
    )
    layer_out = layer(
        attended, hidden, moe_gain, routes.T, w_router.T, w_out.T, w_gate, w_up, w_down
    )
    return (layer_out.astype(jnp.bfloat16), accepted_kv)


def solution(mesh):
    return jax.shard_map(
        local,
        mesh=mesh,
        in_specs=(
            P(("dp", "tp"), None),
            P(),
            P(None, "tp"),
            P(None, "tp"),
            P("tp", None),
            P(("dp", "tp"), None, None),
            P(("dp", "tp"), None, None),
            P(("dp", "tp")),
            P(("dp", "tp"), None),
            P(("dp", "tp")),
            P(),
            P(),
            P("dp", None),
            P("tp", None),
            P("tp", None),
            P("tp", None),
        ),
        out_specs=(P(("dp", "tp"), None), P(("dp", "tp"), None, None)),
        check_vma=False,
    )
```

time: 246 us -> 157 us (0.64)
  local copies, waits for them, and re-layouts: 38.5 us -> 1.93 us
  matrix products: 28.1 us -> 0 us
  other arithmetic: 29.6 us -> 1.63 us
  Pallas kernels: 146 us -> 151 us
    dot_general x8 -> x0, matrix products: 28.1 us -> none  [the longest x1 8.36 us: attend_padded(): jnp.einsum('gqjp,pgd->jgqd', cache_exp.astype(jnp.bfloat16), cache_v, pre...]
    unnamed x33 -> x2, local copies, waits for them, and re-layouts: 16.9 us -> 0.01 us
    pallas_call x2, Pallas kernels: 96.8 us -> 109 us  [the longest x1 98.3 us: layer(): pl.pallas_call(functools.partial(layer_kernel, count), out_shape=jax.Shap...]
    gather x10 -> x0, local copies, waits for them, and re-layouts: 11.9 us -> none  [the longest x1 5.34 us: expert_slots(): picked = inputs[safe]]
    scatter-add x1 -> x0, other arithmetic: 8.74 us -> none  [local(): term = jnp.zeros((count, all_inputs.shape[1]), jnp.float32).at[slot_index...]
    pallas_call x1, Pallas kernels: 49.6 us -> 42.3 us  [project(): pl.pallas_call(functools.partial(project_kernel, count), out_shape=jax.Sh...]
    reduce_sum x6 -> x0, other arithmetic: 6.9 us -> none  [the longest x2 6.57 us: attend_padded(): total = jnp.sum(draft_exp, axis=-1) + jnp.sum(cache_exp, axis=-1)]
    convert_element_type x3 -> x1, other arithmetic: 6.27 us -> 1.63 us  [local(): return (layer_out.astype(jnp.bfloat16), accepted_kv)]
where the time goes in v2:
time: 157 us
  Pallas kernels  151 us (96%)
  between operations  1.96 us (1%)
  local copies, waits for them, and re-layouts  1.93 us (1%)
  other arithmetic  1.63 us (1%)
    pallas_call x1, Pallas kernels, layer(): pl.pallas_call(functools.partial(layer_kernel, count), out_shape=jax.Shap...  98.3 us
    pallas_call x1, Pallas kernels, project(): pl.pallas_call(functools.partial(project_kernel, count), out_shape=jax.Sh...  42.3 us
    pallas_call x1, Pallas kernels, attend(): pl.pallas_call(attend_kernel, out_shape=(jax.ShapeDtypeStruct((count, dra...  10.5 us

profile of v2, /device:TPU:8, one launch (start us, length us, event | category | flops | bytes accessed | tf_op | source)
XLA Modules:
  0.0 156.6 jit_solution(15759539821587137583)
XLA Ops:
  0.6 1.3 reshape.10.gain
  1.9 42.3 %project.1.blocks = bf16[32,24,160]{2,1,0:T(8,128)(2,1)} custom-call(bf16[24,2880]{1,0:T(8,128)(2,1)} %hidden.3, f32[1,2880]{1,0:T(1,128)} %reshape.10.gain, bf16[2880,128]{1,0:T(8,128)(2,1)} %w_query.1, bf16[32,2880]{1,0:T(8,128)(2,1)} %bitcast.5), custom_call_target="tpu_custom_call" | custom-call | tf_op jit(solution)/shard_map/project/pallas_call | solution.py:410
  45.5 0.0 copy-start
  45.5 10.5 %attend.1 = (bf16[32,24,128]{2,1,0:T(8,128)(2,1)}, bf16[1,8,1024]{2,1,0:T(8,128)(2,1)}) custom-call(s32[1]{0:T(128)S(6)} %copy.18.lens, s32[1]{0:T(128)S(6)} %copy.19.leaf, s32[1,24]{1,0:T(1,128)} %parents.1, bf16[32,24,160]{2,1,0:T(8,128)(2,1)} %project.1.blocks, bf16[1,2048,512]{2,1,0:T(8,128)(2,1)} %keys.1, bf16[1,2048,512]{2,1,0:T(8,128)(2,1)} %values.1), custom_call_target="tpu_custom_call" | custom-call | tf_op jit(solution)/shard_map/attend/pallas_call | solution.py:547
  56.0 0.0 copy-done
  56.0 0.6 reshape.11.gain
  56.6 98.3 %layer.1 = f32[24,2880]{1,0:T(8,128)} custom-call(bf16[32,24,128]{2,1,0:T(8,128)(2,1)} %get-tuple-element.4.attended, bf16[24,2880]{1,0:T(8,128)(2,1)} %hidden.3, f32[1,2880]{1,0:T(1,128)} %reshape.11.gain, s32[4,768]{1,0:T(4,128)} %bitcast.7, bf16[32,2880]{1,0:T(8,128)(2,1)} %bitcast.6, bf16[2880,128]{1,0:T(8,128)(2,1)} %bitcast.4, ...), custom_call_target="tpu_custom_call" | custom-call | tf_op jit(solution)/shard_map/layer/pallas_call | solution.py:672
  155.0 1.6 %convert_element_type.3 = bf16[24,2880]{1,0:T(8,128)(2,1)} convert(f32[24,2880]{1,0:T(8,128)} %layer.1) | non-fusion elementwise | flops 69120 | bytes 414720 | tf_op jit(solution)/shard_map/convert_element_type | solution.py:729
Async XLA Ops:
  45.5 10.5 %copy-start = (f32[2880]{0:T(1024)S(1)}, f32[2880]{0:T(1024)}, u32[]{:S(2)}) copy-start(f32[2880]{0:T(1024)} %param.26) | copy-start | bytes 34564
